TPU v7x, 32 devices: a whole 2x2x4 slice. The times are simulated.
32 devices in a mesh: doc: 4 (over z), feat: 8 (over y, x, core).
Axes of the slice: x: 2, y: 2, z: 4, core: 2. Of those that a mesh axis runs over, the one named last changes fastest.
Arguments:
- documents: bfloat16 [512, 512], P('doc', 'feat'), may hold values from -6 to 6
- directions: bfloat16 [512, 32768], P('doc', 'feat'), may hold values from -0.5 to 0.5
- phase: float32 [32768], P('feat'), may hold values from -3.140625 to 3.140625
- amplitude: float32 [32768], P('feat'), may hold values from 0.4 to 2.3
- doc_weight: float32 [512], P('doc'), may hold values from 0.5 to 4.2
- labels: int32 [512], P('doc'), may hold values from 0 to 127
Outputs:
- margins: float32 [512, 128], P('doc')
- scaled_weights: float32 [32768, 128], P('feat')
All inputs are finite; a program needn't handle non-finite values.
Results may differ from a plain program's by a relative error of at most 0.0003.
Values may be sent and summed in bfloat16 or wider, within the bound.
A program may use at most 64 MiB of HBM per device.

v0:
```python
import jax
import jax.numpy as jnp
from jax import lax
from jax.sharding import PartitionSpec as P

C = 128
ITERS = 3
NEWTON = 3
shrink_level = 0.1
ratio_floor = 1e-06


def project_tile(features, factor, start, target):
    residue = target - jnp.dot(features, start, precision=lax.Precision.HIGHEST)
    halfway = lax.linalg.triangular_solve(factor, residue, left_side=True, lower=True)
    solved = lax.linalg.triangular_solve(
        factor, halfway, left_side=True, lower=True, transpose_a=True
    )
    new_copy = start + lax.dot_general(
        features, solved, (((0,), (0,)), ((), ())), precision=lax.Precision.HIGHEST
    )
    new_part = jnp.dot(features, new_copy, precision=lax.Precision.HIGHEST)
    return (new_copy, new_part)


def logistic_prox(target, signs, weight_ratio):
    current = target
    for newton_step in range(NEWTON):
        chance = jax.nn.sigmoid(-signs * current)
        gradient = current - target - weight_ratio * signs * chance
        current = current - gradient / (1.0 + weight_ratio * chance * (1.0 - chance))
    return current


def shrink_values(target, limit):
    return target - jnp.clip(target, -limit, limit)


def per_device(documents, directions, phase, amplitude, doc_weight, labels):
    doc_full = lax.all_gather(documents, "feat", axis=1, tiled=True)
    doc_count = documents.shape[0]
    width_tile = directions.shape[1]
    num_feat = lax.axis_size("feat")
    num_doc = lax.axis_size("doc")
    angles = jnp.dot(
        doc_full,
        lax.all_gather(directions, "doc", axis=0, tiled=True),
        preferred_element_type=jnp.float32,
    )
    features = jnp.sqrt(2.0 / width_tile) * amplitude * jnp.cos(angles + phase)
    gram = jnp.eye(doc_count, dtype=jnp.float32) + lax.dot_general(
        features, features, (((1,), (1,)), ((), ())), precision=lax.Precision.HIGHEST
    )
    factor = jnp.linalg.cholesky(gram)
    signs = jnp.where(labels[:, None] == jnp.arange(C, dtype=jnp.int32)[None, :], 1.0, -1.0).astype(
        jnp.float32
    )
    share_rows = doc_count // num_feat
    offset = lax.axis_index("feat") * share_rows
    local_signs = lax.dynamic_slice_in_dim(signs, offset, share_rows, 0)
    local_weight = lax.dynamic_slice_in_dim(doc_weight, offset, share_rows, 0)[:, None]
    rho = jnp.float32(1.0)
    margins = logistic_prox(
        jnp.zeros(local_signs.shape, jnp.float32), local_signs, local_weight / rho
    )
    sums = jnp.zeros(local_signs.shape, jnp.float32)
    duals_y = jnp.zeros(local_signs.shape, jnp.float32)
    duals_x = jnp.zeros((width_tile, C), jnp.float32)
    partial_value = jnp.zeros((doc_count, C), jnp.float32)
    weights = jnp.zeros((width_tile, C), jnp.float32)
    for step in range(ITERS):
        correction = (margins - duals_y - sums) / num_feat
        correction = lax.all_gather(correction, "feat", axis=0, tiled=True)
        new_copy, partial_value = project_tile(
            features, factor, weights - duals_x, partial_value + correction
        )
        sums = lax.psum_scatter(partial_value, "feat", scatter_dimension=0, tiled=True)
        old_weights = weights
        old_margins = margins
        limit = shrink_level / (rho * num_doc)
        summed = lax.psum(new_copy + duals_x, "doc")
        weights = shrink_values(summed / num_doc, limit)
        margins = logistic_prox(sums + duals_y, local_signs, local_weight / rho)
        duals_x = duals_x + new_copy - weights
        duals_y = duals_y + sums - margins
        if step + 1 < ITERS:
            margin_gap = jnp.sum((sums - margins) ** 2)
            margin_move = jnp.sum((margins - old_margins) ** 2)
            primal, dual_norm = lax.psum(
                (
                    jnp.sum((new_copy - weights) ** 2) + margin_gap,
                    jnp.sum((weights - old_weights) ** 2) + margin_move,
                ),
                ("doc", "feat"),
            )
            dual_norm = rho * rho * dual_norm
            growth = ((primal + ratio_floor) / (dual_norm + ratio_floor)) ** 0.25
            rho = rho * growth
            duals_x = duals_x / growth
            duals_y = duals_y / growth
    margins = lax.all_gather(margins, "feat", axis=0, tiled=True)
    return (margins, num_feat * weights)


def solution(mesh):
    in_specs = (P("doc", "feat"), P("doc", "feat"), P("feat"), P("feat"), P("doc"), P("doc"))
    out_specs = (P("doc", None), P("feat", None))
    return jax.shard_map(
        per_device, mesh=mesh, in_specs=in_specs, out_specs=out_specs, check_vma=False
    )
```

profile of v0, /device:TPU:0, one launch (start us, length us, event | category | flops | bytes accessed | tf_op | source)
XLA Modules:
  0.0 668.8 jit_solution(7295771002411407596)
XLA Ops:
  9.6 10.7 %all_gather.20 = f32[128,128]{1,0:T(8,128)S(1)} all-gather(f32[16,128]{1,0:T(8,128)S(1)} %broadcast_multiply_fusion.1), channel_id=1, replica_groups=mesh['doc'=4,'feat'=8] {'feat'}, dimensions={0}, use_global_device_ids=true | all-gather | bytes 73728 | tf_op jit(solution)/shard_map/all_gather | solution.py:73
  20.3 9.2 %all_gather.18 = bf16[128,512]{0,1:T(8,128)(2,1)S(1)} all-gather(bf16[128,64]{0,1:T(8,128)(2,1)} %param.10), channel_id=1, replica_groups=mesh['doc'=4,'feat'=8] {'feat'}, dimensions={1}, use_global_device_ids=true | all-gather | bytes 147456 | tf_op jit(solution)/shard_map/all_gather | solution.py:40
  30.2 62.9 %all-gather.2.cloned.1.call-done = bf16[512,4096]{1,0:T(8,128)(2,1)} async-done(((bf16[128,4096]{1,0:T(8,128)(2,1)}), bf16[512,4096]{1,0:T(8,128)(2,1)}) %all-gather.2.cloned.1.call-update) | async-done | bytes 4194320 | tf_op jit(solution)/shard_map/all_gather | solution.py:47
  93.0 9.5 %fusion.1 = f32[128,4096]{1,0:T(8,128)S(1)} fusion(bf16[128,512]{0,1:T(8,128)(2,1)S(1)} %all_gather.18, bf16[512,4096]{1,0:T(8,128)(2,1)} %all-gather.2.cloned.1.call-done, f32[4096]{0:T(1024)} %param.12, f32[4096]{0:T(1024)S(1)} %broadcast_multiply_fusion), kind=kOutput, calls=%fused_computation.4 | convolution fusion | flops 537919488 | bytes 6455296 | tf_op jit(solution)/shard_map/dot_general | solution.py:45
  102.5 1.8 fusion.140
  104.3 1.8 convolution_subtract_fusion.2
  106.2 11.7 %cholesky.20 = f32[128,128]{1,0:T(8,128)S(1)} custom-call(f32[128,128]{1,0:T(8,128)S(1)} %fusion.22), custom_call_target="Cholesky" | custom-call | tf_op jit(solution)/shard_map/jit(cholesky)/cholesky | solution.py:54
  119.3 9.8 %custom-call.14 = f32[1,128,128]{1,2,0:T(8,128)S(1)} custom-call(f32[1,128,128]{2,1,0:T(8,128)S(1)} %fusion.8), custom_call_target="InvertDiagBlocksLowerTriangular" | custom-call | tf_op jit(solution)/shard_map/triangular_solve/custom-call.2 | solution.py:16
  129.6 16.5 %fusion.141 = f32[4096,128]{1,0:T(8,128)} fusion(f32[128,4096]{1,0:T(8,128)S(1)} %fusion.1, f32[128,128]{1,0:T(8,128)S(1)} %fusion.19), kind=kOutput, calls=%fused_computation.176 | convolution fusion | flops 805306368 | bytes 4259840 | tf_op jit(solution)/shard_map/dot_general | solution.py:19
  146.1 4.4 fusion.142
  151.2 31.4 %reduce-scatter.4.cloned.1.call-done = f32[16,128]{1,0:T(8,128)} async-done(((f32[128,128]{1,0:T(8,128)}), f32[16,128]{1,0:T(8,128)}) %reduce-scatter.4.cloned.1.call-update) | async-done | bytes 8208 | tf_op jit(solution)/shard_map/reduce_scatter | solution.py:77
  182.6 1.5 multiply_reduce_fusion.6
  185.5 86.3 %all-reduce.6.cloned.1.call-done = f32[4096,128]{1,0:T(8,128)} async-done(((f32[4096,128]{1,0:T(8,128)}), f32[4096,128]{1,0:T(8,128)}) %all-reduce.6.cloned.1.call-update) | async-done | bytes 2097168 | tf_op jit(solution)/shard_map/psum | solution.py:81
  271.8 3.4 multiply_reduce_fusion.2
  277.5 39.3 %all-reduce.1 = (f32[]{:T(128)}, f32[]{:T(128)}) all-reduce(f32[]{:T(128)S(6)} %add.189, f32[]{:T(128)S(6)} %add.191), channel_id=1, replica_groups=mesh['doc'=4,'feat'=8] {'doc','feat'}, use_global_device_ids=true, to_apply=%region_6.9 | all-reduce | flops 2 | bytes 16 | tf_op jit(solution)/shard_map/psum | solution.py:89
  318.2 10.2 %all_gather.21 = f32[128,128]{1,0:T(8,128)S(1)} all-gather(f32[16,128]{1,0:T(8,128)S(1)} %subtract_multiply_fusion.2), channel_id=1, replica_groups=mesh['doc'=4,'feat'=8] {'feat'}, dimensions={0}, use_global_device_ids=true | all-gather | bytes 73728 | tf_op jit(solution)/shard_map/all_gather | solution.py:73
  328.4 4.9 convolution_subtract_fusion.1
  333.8 5.1 fusion.5
  340.2 2.8 fusion.143
  343.8 31.9 %reduce-scatter.6.cloned.1.call-done = f32[16,128]{1,0:T(8,128)} async-done(((f32[128,128]{1,0:T(8,128)}), f32[16,128]{1,0:T(8,128)}) %reduce-scatter.6.cloned.1.call-update) | async-done | bytes 8208 | tf_op jit(solution)/shard_map/reduce_scatter | solution.py:77
  375.7 1.5 multiply_reduce_fusion.4
  377.2 87.4 %all-reduce.8.cloned.1.call-done = f32[4096,128]{1,0:T(8,128)} async-done(((f32[4096,128]{1,0:T(8,128)}), f32[4096,128]{1,0:T(8,128)}) %all-reduce.8.cloned.1.call-update) | async-done | bytes 2097168 | tf_op jit(solution)/shard_map/psum | solution.py:81
  464.7 4.4 multiply_reduce_fusion
  471.5 39.3 %all-reduce = (f32[]{:T(128)}, f32[]{:T(128)}) all-reduce(f32[]{:T(128)S(6)} %add.203, f32[]{:T(128)S(6)} %add.205), channel_id=1, replica_groups=mesh['doc'=4,'feat'=8] {'doc','feat'}, use_global_device_ids=true, to_apply=%region_14.17 | all-reduce | flops 2 | bytes 16 | tf_op jit(solution)/shard_map/psum | solution.py:89
  512.2 10.5 %all_gather.22 = f32[128,128]{1,0:T(8,128)S(1)} all-gather(f32[16,128]{1,0:T(8,128)S(1)} %subtract_multiply_fusion.1), channel_id=1, replica_groups=mesh['doc'=4,'feat'=8] {'feat'}, dimensions={0}, use_global_device_ids=true | all-gather | bytes 73728 | tf_op jit(solution)/shard_map/all_gather | solution.py:73
  522.7 5.0 convolution_subtract_fusion
  528.2 5.1 fusion.6
  533.3 2.8 fusion.144
  537.0 31.8 %reduce-scatter.8.cloned.1.call-done = f32[16,128]{1,0:T(8,128)} async-done(((f32[128,128]{1,0:T(8,128)}), f32[16,128]{1,0:T(8,128)}) %reduce-scatter.8.cloned.1.call-update) | async-done | bytes 8208 | tf_op jit(solution)/shard_map/reduce_scatter | solution.py:77
  569.6 9.2 %all_gather.23 = f32[128,128]{1,0:T(8,128)S(1)} all-gather(f32[16,128]{1,0:T(8,128)S(1)} %fusion.64), channel_id=1, replica_groups=mesh['doc'=4,'feat'=8] {'feat'}, dimensions={0}, use_global_device_ids=true | all-gather | bytes 73728 | tf_op jit(solution)/shard_map/all_gather | solution.py:101
  578.8 79.0 %all-reduce.10.cloned.1.call-done = f32[4096,128]{1,0:T(8,128)} async-done(((f32[4096,128]{1,0:T(8,128)}), f32[4096,128]{1,0:T(8,128)}) %all-reduce.10.cloned.1.call-update) | async-done | bytes 2097168 | tf_op jit(solution)/shard_map/psum | solution.py:81
  657.9 3.2 subtract_multiply_fusion
  (56 shorter events, 12.5 us)
Async XLA Ops:
  7.2 85.9 %all-gather.2.cloned.1.call-start = ((), (), s32[]{:S(2)}) async-start(), calls=%async_computation.3 | async-start | bytes 5242880 | tf_op jit(solution)/shard_map/all_gather | solution.py:47
  7.9 174.7 %reduce-scatter.4.cloned.1.call-start = ((), (), s32[]{:S(2)}) async-start(), calls=%async_computation.5 | async-start | bytes 73728 | tf_op jit(solution)/shard_map/reduce_scatter | solution.py:77
  150.5 121.3 %all-reduce.6.cloned.1.call-start = ((), (), s32[]{:S(2)}) async-start(), calls=%async_computation.4 | async-start | bytes 4194304 | tf_op jit(solution)/shard_map/psum | solution.py:81
  151.2 224.5 %reduce-scatter.6.cloned.1.call-start = ((), (), s32[]{:S(2)}) async-start(), calls=%async_computation.7 | async-start | bytes 73728 | tf_op jit(solution)/shard_map/reduce_scatter | solution.py:77
  185.5 132.7 %copy-start.8 = (f32[16,128]{1,0:T(8,128)S(1)}, f32[16,128]{1,0:T(8,128)}, u32[]{:S(2)}) copy-start(f32[16,128]{1,0:T(8,128)} %reduce-scatter.4.cloned.1.call-done) | copy-start | bytes 24580
  185.5 142.9 %copy-start.6 = (f32[128,128]{1,0:T(8,128)S(1)}, f32[128,128]{1,0:T(8,128)}, u32[]{:S(2)}) copy-start(f32[128,128]{1,0:T(8,128)} %fusion.142) | copy-start | bytes 196612
  328.4 5.4 copy-start
  328.4 5.4 copy-start.1
  338.9 1.3 copy-start.2
  343.0 0.7 copy-start.9
  343.0 121.6 %all-reduce.8.cloned.1.call-start = ((), (), s32[]{:S(2)}) async-start(), calls=%async_computation.6 | async-start | bytes 4194304 | tf_op jit(solution)/shard_map/psum | solution.py:81
  343.6 225.2 %reduce-scatter.8.cloned.1.call-start = ((), (), s32[]{:S(2)}) async-start(), calls=%async_computation.8 | async-start | bytes 73728 | tf_op jit(solution)/shard_map/reduce_scatter | solution.py:77
  377.2 135.0 %copy-start.7 = (f32[16,128]{1,0:T(8,128)S(1)}, f32[16,128]{1,0:T(8,128)}, u32[]{:S(2)}) copy-start(f32[16,128]{1,0:T(8,128)} %reduce-scatter.6.cloned.1.call-done) | copy-start | bytes 24580
  377.2 145.4 %copy-start.5 = (f32[128,128]{1,0:T(8,128)S(1)}, f32[128,128]{1,0:T(8,128)}, u32[]{:S(2)}) copy-start(f32[128,128]{1,0:T(8,128)} %fusion.143) | copy-start | bytes 196612
  522.7 5.5 copy-start.3
  522.7 5.5 copy-start.4
  536.1 121.8 %all-reduce.10.cloned.1.call-start = ((), (), s32[]{:S(2)}) async-start(), calls=%async_computation.9 | async-start | bytes 4194304 | tf_op jit(solution)/shard_map/psum | solution.py:81
Sparse Core Ops, SparseCore 0:
  9.5 83.4 all-gather.1
  150.6 32.0 reduce-scatter.3
  185.6 86.1 all-reduce.5
  343.2 32.5 reduce-scatter.5
  378.5 86.0 all-reduce.7
  536.2 32.5 reduce-scatter.7
  571.7 86.0 all-reduce.9
where the time goes:
time: 673 us; the launch traced here: 669 us
  waiting for transfers between devices  413 us (61%)
  blocking collectives  128 us (19%)
  matrix products  61 us (9%)
  other arithmetic  40.1 us (6%)
  between operations  22.2 us (3%)
    psum x3, waiting for transfers between devices, per_device(): summed = lax.psum(new_copy + duals_x, 'doc')  253 us
    reduce_scatter x3, waiting for transfers between devices, per_device(): lax.psum_scatter(partial_value, 'feat', scatter_dimension=0, tiled=True)  95.1 us
    psum x2, blocking collectives, per_device(): lax.psum((jnp.sum((new_copy - weights) ** 2) + margin_gap, jnp.sum((weigh...  78.6 us
    all_gather x1, waiting for transfers between devices, per_device(): lax.all_gather(directions, 'doc', axis=0, tiled=True)  62.9 us
    all_gather x3, blocking collectives, per_device(): correction = lax.all_gather(correction, 'feat', axis=0, tiled=True)  31.4 us
    dot_general x3, matrix products, project_tile(): lax.dot_general(features, solved, (((0,), (0,)), ((), ())), precision=lax...  26.6 us
  transfers between devices with their start and end apart: 7, of which 7 were waited for; matrix products, arithmetic and copies ran while one was open for 1% of the time, Pallas kernels for 0%

commit v1 on v0

--- a/solution.py
+++ b/solution.py
@@ -8,6 +8,16 @@
 NEWTON = 3
 shrink_level = 0.1
 ratio_floor = 1e-06
+
+
+def ring_gather(x, axis, dim):
+    ways, here, step = (lax.axis_size(axis), lax.axis_index(axis), x.shape[dim])
+    shape = [n * ways if d == dim else n for d, n in enumerate(x.shape)]
+    full = lax.dynamic_update_slice_in_dim(jnp.zeros(shape, x.dtype), x, here * step, axis=dim)
+    for far in range(1, ways):
+        x = lax.ppermute(x, axis, [(d, (d + 1) % ways) for d in range(ways)])
+        full = lax.dynamic_update_slice_in_dim(full, x, (here - far) % ways * step, axis=dim)
+    return full
 
 
 def project_tile(features, factor, start, target):
@@ -43,9 +53,7 @@
     num_feat = lax.axis_size("feat")
     num_doc = lax.axis_size("doc")
     angles = jnp.dot(
-        doc_full,
-        lax.all_gather(directions, "doc", axis=0, tiled=True),
-        preferred_element_type=jnp.float32,
+        doc_full, ring_gather(directions, "doc", 0), preferred_element_type=jnp.float32
     )
     features = jnp.sqrt(2.0 / width_tile) * amplitude * jnp.cos(angles + phase)
     gram = jnp.eye(doc_count, dtype=jnp.float32) + lax.dot_general(

time: 673 us -> 563 us (0.84)
  waiting for transfers between devices: 413 us -> 300 us
    psum x3, waiting for transfers between devices: 253 us -> 153 us  [per_device(): summed = lax.psum(new_copy + duals_x, 'doc')]
    all_gather x1 -> x0, waiting for transfers between devices: 62.9 us -> none  [per_device(): lax.all_gather(directions, 'doc', axis=0, tiled=True)]
    ppermute x0 -> x3, waiting for transfers between devices: none -> 50.6 us  [ring_gather(): x = lax.ppermute(x, axis, [(d, (d + 1) % ways) for d in range(ways)])]
    dot_general x3, matrix products: 26.6 us -> 10.1 us  [project_tile(): lax.dot_general(features, solved, (((0,), (0,)), ((), ())), precision=lax...]
  transfers between devices with their start and end apart: 7 -> 9, of which waited for: 7 -> 9; matrix products, arithmetic and copies ran while one was open for 1% -> 2% of each run, Pallas kernels for 0% -> 0%
where the time goes in v1:
time: 563 us; the launch traced here: 559 us
  waiting for transfers between devices  300 us (53%)
  blocking collectives  127 us (23%)
  matrix products  55 us (10%)
  other arithmetic  40.3 us (7%)
  between operations  23.5 us (4%)
  local copies, waits for them, and re-layouts  10.2 us (2%)
    psum x3, waiting for transfers between devices, per_device(): summed = lax.psum(new_copy + duals_x, 'doc')  153 us
    reduce_scatter x3, waiting for transfers between devices, per_device(): lax.psum_scatter(partial_value, 'feat', scatter_dimension=0, tiled=True)  94.7 us
    psum x2, blocking collectives, per_device(): lax.psum((jnp.sum((new_copy - weights) ** 2) + margin_gap, jnp.sum((weigh...  78.8 us
    ppermute x3, waiting for transfers between devices, ring_gather(): x = lax.ppermute(x, axis, [(d, (d + 1) % ways) for d in range(ways)])  50.6 us
    all_gather x3, blocking collectives, per_device(): correction = lax.all_gather(correction, 'feat', axis=0, tiled=True)  30 us
    dot_general x3, matrix products, project_tile(): residue = target - jnp.dot(features, start, precision=lax.Precision.HIGHEST)  15.8 us
    dot_general x3, matrix products, project_tile(): new_part = jnp.dot(features, new_copy, precision=lax.Precision.HIGHEST)  13.9 us
    another operation x3, other arithmetic, per_device(): factor = jnp.linalg.cholesky(gram)  12.4 us
  transfers between devices with their start and end apart: 9, of which 9 were waited for; matrix products, arithmetic and copies ran while one was open for 2% of the time, Pallas kernels for 0%

profile of v1, /device:TPU:0, one launch (start us, length us, event | category | flops | bytes accessed | tf_op | source)
XLA Modules:
  0.0 559.2 jit_solution(318528297586975134)
XLA Ops:
  11.1 25.4 %collective-permute-done = bf16[128,4096]{1,0:T(8,128)(2,1)S(1)} collective-permute-done((bf16[128,4096]{1,0:T(8,128)(2,1)}, bf16[128,4096]{1,0:T(8,128)(2,1)S(1)}, u32[]{:S(2)}, u32[]{:S(2)}) %collective-permute-start) | collective-permute-done | bytes 1048608 | tf_op jit(solution)/shard_map/ppermute | solution.py:18
  42.2 20.4 %collective-permute-done.1 = bf16[128,4096]{1,0:T(8,128)(2,1)S(1)} collective-permute-done((bf16[128,4096]{1,0:T(8,128)(2,1)S(1)}, bf16[128,4096]{1,0:T(8,128)(2,1)S(1)}, u32[]{:S(2)}, u32[]{:S(2)}) %collective-permute-start.1) | collective-permute-done | bytes 1048608 | tf_op jit(solution)/shard_map/ppermute | solution.py:18
  62.9 9.0 %all_gather.16 = f32[128,128]{1,0:T(8,128)S(1)} all-gather(f32[16,128]{1,0:T(8,128)S(1)} %broadcast_multiply_fusion.1), channel_id=1, replica_groups=mesh['doc'=4,'feat'=8] {'feat'}, dimensions={0}, use_global_device_ids=true | all-gather | bytes 73728 | tf_op jit(solution)/shard_map/all_gather | solution.py:81
  71.9 9.2 %all_gather.15 = bf16[128,512]{0,1:T(8,128)(2,1)S(1)} all-gather(bf16[128,64]{0,1:T(8,128)(2,1)S(1)} %copy-done.11), channel_id=1, replica_groups=mesh['doc'=4,'feat'=8] {'feat'}, dimensions={1}, use_global_device_ids=true | all-gather | bytes 147456 | tf_op jit(solution)/shard_map/all_gather | solution.py:50
  83.2 4.7 collective-permute-done.2
  89.0 10.2 %fusion.1 = f32[4096,128]{1,0:T(8,128)S(1)} fusion(bf16[512,4096]{1,0:T(8,128)(2,1)} %constant_dynamic-update-slice_fusion, bf16[128,512]{0,1:T(8,128)(2,1)S(1)} %all_gather.15, f32[4096]{0:T(1024)S(1)} %copy-done.8, f32[4096]{0:T(1024)S(1)} %broadcast_multiply_fusion), kind=kOutput, calls=%fused_computation.4 | convolution fusion | flops 537919488 | bytes 6455296 | tf_op jit(solution)/shard_map/dot_general | solution.py:55
  99.3 3.5 fusion.140
  102.7 3.4 convolution_subtract_fusion.2
  106.3 11.7 %cholesky.20 = f32[128,128]{1,0:T(8,128)S(1)} custom-call(f32[128,128]{1,0:T(8,128)S(1)} %fusion.22), custom_call_target="Cholesky" | custom-call | tf_op jit(solution)/shard_map/jit(cholesky)/cholesky | solution.py:62
  119.3 10.0 %custom-call.14 = f32[1,128,128]{1,2,0:T(8,128)S(1)} custom-call(f32[1,128,128]{2,1,0:T(8,128)S(1)} %fusion.8), custom_call_target="InvertDiagBlocksLowerTriangular" | custom-call | tf_op jit(solution)/shard_map/triangular_solve/custom-call.2 | solution.py:26
  129.8 3.1 fusion.141
  133.0 5.7 %fusion.142 = f32[128,128]{1,0:T(8,128)} fusion(f32[4096,128]{1,0:T(8,128)S(1)} %fusion.1, f32[4096,128]{1,0:T(8,128)} %fusion.141), kind=kOutput, calls=%fused_computation.181 | convolution fusion | flops 805306368 | bytes 4259840 | tf_op jit(solution)/shard_map/dot_general | solution.py:32
  139.3 30.8 %reduce-scatter.4.cloned.1.call-done = f32[16,128]{1,0:T(8,128)} async-done(((f32[128,128]{1,0:T(8,128)}), f32[16,128]{1,0:T(8,128)}) %reduce-scatter.4.cloned.1.call-update) | async-done | bytes 8208 | tf_op jit(solution)/shard_map/reduce_scatter | solution.py:85
  172.9 52.9 %all-reduce.6.cloned.1.call-done = f32[4096,128]{1,0:T(8,128)} async-done(((f32[4096,128]{1,0:T(8,128)}), f32[4096,128]{1,0:T(8,128)}) %all-reduce.6.cloned.1.call-update) | async-done | bytes 2097168 | tf_op jit(solution)/shard_map/psum | solution.py:89
  225.8 3.4 multiply_reduce_fusion.2
  231.6 39.3 %all-reduce.1 = (f32[]{:T(128)}, f32[]{:T(128)}) all-reduce(f32[]{:T(128)S(6)} %add.222, f32[]{:T(128)S(6)} %add.224), channel_id=1, replica_groups=mesh['doc'=4,'feat'=8] {'doc','feat'}, use_global_device_ids=true, to_apply=%region_6.9 | all-reduce | flops 2 | bytes 16 | tf_op jit(solution)/shard_map/psum | solution.py:97
  272.2 10.6 %all_gather.17 = f32[128,128]{1,0:T(8,128)S(1)} all-gather(f32[16,128]{1,0:T(8,128)S(1)} %subtract_multiply_fusion.2), channel_id=1, replica_groups=mesh['doc'=4,'feat'=8] {'feat'}, dimensions={0}, use_global_device_ids=true | all-gather | bytes 73728 | tf_op jit(solution)/shard_map/all_gather | solution.py:81
  282.9 6.2 %convolution_subtract_fusion.1 = f32[128,128]{1,0:T(8,128)S(1)} fusion(f32[4096,128]{1,0:T(8,128)S(1)} %fusion.1, f32[128,128]{1,0:T(8,128)S(1)} %copy-done.7, f32[128,128]{1,0:T(8,128)S(1)} %all_gather.17, f32[4096,128]{1,0:T(8,128)} %all-reduce.6.cloned.1.call-done, f32[]{:T(128)S(6)} %pow.6, f32[4096,128]{1,0:T(8,128)} %fusion.141), kind=kOutput, calls=%fused_computation.14 | convolution fusion | flops 808484864 | bytes 6488068 | tf_op jit(solution)/shard_map/dot_general | solution.py:24
  289.6 3.5 fusion.5
  294.4 4.1 fusion.143
  299.3 31.9 %reduce-scatter.6.cloned.1.call-done = f32[16,128]{1,0:T(8,128)} async-done(((f32[128,128]{1,0:T(8,128)}), f32[16,128]{1,0:T(8,128)}) %reduce-scatter.6.cloned.1.call-update) | async-done | bytes 8208 | tf_op jit(solution)/shard_map/reduce_scatter | solution.py:85
  332.7 54.2 %all-reduce.8.cloned.1.call-done = f32[4096,128]{1,0:T(8,128)} async-done(((f32[4096,128]{1,0:T(8,128)}), f32[4096,128]{1,0:T(8,128)}) %all-reduce.8.cloned.1.call-update) | async-done | bytes 2097168 | tf_op jit(solution)/shard_map/psum | solution.py:89
  386.9 4.4 multiply_reduce_fusion
  393.8 39.5 %all-reduce = (f32[]{:T(128)}, f32[]{:T(128)}) all-reduce(f32[]{:T(128)S(6)} %add.236, f32[]{:T(128)S(6)} %add.238), channel_id=1, replica_groups=mesh['doc'=4,'feat'=8] {'doc','feat'}, use_global_device_ids=true, to_apply=%region_14.17 | all-reduce | flops 2 | bytes 16 | tf_op jit(solution)/shard_map/psum | solution.py:97
  434.6 10.3 %all_gather.18 = f32[128,128]{1,0:T(8,128)S(1)} all-gather(f32[16,128]{1,0:T(8,128)S(1)} %subtract_multiply_fusion.1), channel_id=1, replica_groups=mesh['doc'=4,'feat'=8] {'feat'}, dimensions={0}, use_global_device_ids=true | all-gather | bytes 73728 | tf_op jit(solution)/shard_map/all_gather | solution.py:81
  444.9 6.2 %convolution_subtract_fusion = f32[128,128]{1,0:T(8,128)S(1)} fusion(f32[4096,128]{1,0:T(8,128)S(1)} %fusion.1, f32[128,128]{1,0:T(8,128)S(1)} %copy-done.6, f32[128,128]{1,0:T(8,128)S(1)} %all_gather.18, f32[]{:T(128)S(6)} %pow.7, f32[4096,128]{1,0:T(8,128)} %get-tuple-element.19, f32[]{:T(128)S(6)} %neg.63, f32[]{:T(128)S(6)} %div.173, ...), kind=kOutput, calls=%fused_computation.13 | convolution fusion | flops 809009152 | bytes 6488076 | tf_op jit(solution)/shard_map/dot_general | solution.py:24
  451.7 3.5 fusion.6
  455.2 4.1 fusion.144
  460.1 32.0 %reduce-scatter.8.cloned.1.call-done = f32[16,128]{1,0:T(8,128)} async-done(((f32[128,128]{1,0:T(8,128)}), f32[16,128]{1,0:T(8,128)}) %reduce-scatter.8.cloned.1.call-update) | async-done | bytes 8208 | tf_op jit(solution)/shard_map/reduce_scatter | solution.py:85
  492.9 9.2 %all_gather.19 = f32[128,128]{1,0:T(8,128)S(1)} all-gather(f32[16,128]{1,0:T(8,128)S(1)} %fusion.64), channel_id=1, replica_groups=mesh['doc'=4,'feat'=8] {'feat'}, dimensions={0}, use_global_device_ids=true | all-gather | bytes 73728 | tf_op jit(solution)/shard_map/all_gather | solution.py:109
  502.1 45.7 %all-reduce.10.cloned.1.call-done = f32[4096,128]{1,0:T(8,128)} async-done(((f32[4096,128]{1,0:T(8,128)}), f32[4096,128]{1,0:T(8,128)}) %all-reduce.10.cloned.1.call-update) | async-done | bytes 2097168 | tf_op jit(solution)/shard_map/psum | solution.py:89
  547.8 3.2 subtract_multiply_fusion
  (70 shorter events, 24.3 us)
Async XLA Ops:
  8.0 162.1 %reduce-scatter.4.cloned.1.call-start = ((), (), s32[]{:S(2)}) async-start(), calls=%async_computation.4 | async-start | bytes 73728 | tf_op jit(solution)/shard_map/reduce_scatter | solution.py:85
  8.0 28.5 %collective-permute-start = (bf16[128,4096]{1,0:T(8,128)(2,1)}, bf16[128,4096]{1,0:T(8,128)(2,1)S(1)}, u32[]{:S(2)}, u32[]{:S(2)}) collective-permute-start(bf16[128,4096]{1,0:T(8,128)(2,1)} %param.11), channel_id=1, source_target_pairs={{0,8},{8,16},{16,24},{24,0},{1,9},{9,17},{17,25},{25,1},{2,10},{10... | collective-permute-start | bytes 3145736 | tf_op jit(solution)/shard_map/ppermute | solution.py:18
  36.5 26.1 %collective-permute-start.1 = (bf16[128,4096]{1,0:T(8,128)(2,1)S(1)}, bf16[128,4096]{1,0:T(8,128)(2,1)S(1)}, u32[]{:S(2)}, u32[]{:S(2)}) collective-permute-start(bf16[128,4096]{1,0:T(8,128)(2,1)S(1)} %collective-permute-done), channel_id=1, source_target_pairs={{0,8},{8,16},{16,24},{24,0},{1,9},{9,17},{17,25},{25,1},{2,10},{10... | collective-permute-start | bytes 3145736 | tf_op jit(solution)/shard_map/ppermute | solution.py:18
  38.7 2.4 copy-start.5
  41.2 30.8 %copy-start.11 = (bf16[128,64]{0,1:T(8,128)(2,1)S(1)}, bf16[128,64]{0,1:T(8,128)(2,1)}, u32[]{:S(2)}) copy-start(bf16[128,64]{0,1:T(8,128)(2,1)} %param.10) | copy-start | bytes 49156
  62.7 25.3 %collective-permute-start.2 = (bf16[128,4096]{1,0:T(8,128)(2,1)S(1)}, bf16[128,4096]{1,0:T(8,128)(2,1)S(1)}, u32[]{:S(2)}, u32[]{:S(2)}) collective-permute-start(bf16[128,4096]{1,0:T(8,128)(2,1)S(1)} %collective-permute-done.1), channel_id=1, source_target_pairs={{0,8},{8,16},{16,24},{24,0},{1,9},{9,17},{17,25},{25,1},{2,10},{10... | collective-permute-start | bytes 3145736 | tf_op jit(solution)/shard_map/ppermute | solution.py:18
  82.1 6.9 %copy-start.8 = (f32[4096]{0:T(1024)S(1)}, f32[4096]{0:T(1024)}, u32[]{:S(2)}) copy-start(f32[4096]{0:T(1024)} %param.12) | copy-start | bytes 49156
  138.6 87.2 %all-reduce.6.cloned.1.call-start = ((), (), s32[]{:S(2)}) async-start(), calls=%async_computation.3 | async-start | bytes 4194304 | tf_op jit(solution)/shard_map/psum | solution.py:89
  139.2 192.0 %reduce-scatter.6.cloned.1.call-start = ((), (), s32[]{:S(2)}) async-start(), calls=%async_computation.6 | async-start | bytes 73728 | tf_op jit(solution)/shard_map/reduce_scatter | solution.py:85
  172.9 99.3 %copy-start.10 = (f32[16,128]{1,0:T(8,128)S(1)}, f32[16,128]{1,0:T(8,128)}, u32[]{:S(2)}) copy-start(f32[16,128]{1,0:T(8,128)} %reduce-scatter.4.cloned.1.call-done) | copy-start | bytes 24580
  172.9 109.9 %copy-start.7 = (f32[128,128]{1,0:T(8,128)S(1)}, f32[128,128]{1,0:T(8,128)}, u32[]{:S(2)}) copy-start(f32[128,128]{1,0:T(8,128)} %fusion.142) | copy-start | bytes 196612
  282.9 6.7 %copy-start = (f32[4096,128]{1,0:T(8,128)S(1)}, f32[4096,128]{1,0:T(8,128)}, u32[]{:S(2)}) copy-start(f32[4096,128]{1,0:T(8,128)} %fusion.141) | copy-start | bytes 6291460
  282.9 6.7 %copy-start.1 = (f32[4096,128]{1,0:T(8,128)S(1)}, f32[4096,128]{1,0:T(8,128)}, u32[]{:S(2)}) copy-start(f32[4096,128]{1,0:T(8,128)} %all-reduce.6.cloned.1.call-done) | copy-start | bytes 6291460
  293.1 1.3 copy-start.2
  298.5 0.7 copy-start.12
  298.5 88.4 %all-reduce.8.cloned.1.call-start = ((), (), s32[]{:S(2)}) async-start(), calls=%async_computation.5 | async-start | bytes 4194304 | tf_op jit(solution)/shard_map/psum | solution.py:89
  299.1 192.9 %reduce-scatter.8.cloned.1.call-start = ((), (), s32[]{:S(2)}) async-start(), calls=%async_computation.7 | async-start | bytes 73728 | tf_op jit(solution)/shard_map/reduce_scatter | solution.py:85
  332.7 101.9 %copy-start.9 = (f32[16,128]{1,0:T(8,128)S(1)}, f32[16,128]{1,0:T(8,128)}, u32[]{:S(2)}) copy-start(f32[16,128]{1,0:T(8,128)} %reduce-scatter.6.cloned.1.call-done) | copy-start | bytes 24580
  332.7 112.2 %copy-start.6 = (f32[128,128]{1,0:T(8,128)S(1)}, f32[128,128]{1,0:T(8,128)}, u32[]{:S(2)}) copy-start(f32[128,128]{1,0:T(8,128)} %fusion.143) | copy-start | bytes 196612
  444.9 6.8 %copy-start.3 = (f32[4096,128]{1,0:T(8,128)S(1)}, f32[4096,128]{1,0:T(8,128)}, u32[]{:S(2)}) copy-start(f32[4096,128]{1,0:T(8,128)} %get-tuple-element.19) | copy-start | bytes 6291460
  444.9 6.8 %copy-start.4 = (f32[4096,128]{1,0:T(8,128)S(1)}, f32[4096,128]{1,0:T(8,128)}, u32[]{:S(2)}) copy-start(f32[4096,128]{1,0:T(8,128)} %all-reduce.8.cloned.1.call-done) | copy-start | bytes 6291460
  459.4 88.4 %all-reduce.10.cloned.1.call-start = ((), (), s32[]{:S(2)}) async-start(), calls=%async_computation.8 | async-start | bytes 4194304 | tf_op jit(solution)/shard_map/psum | solution.py:89
Sparse Core Ops, SparseCore 0:
  138.8 31.2 reduce-scatter.3
  298.6 32.5 reduce-scatter.5
  459.5 32.5 reduce-scatter.7
Sparse Core Ops, SparseCore 1:
  142.1 83.7 all-reduce.5
  302.0 84.9 all-reduce.7
  462.8 84.9 all-reduce.9
